TPU v7x, 32 devices: a whole 2x2x4 slice. The times are simulated.
32 devices in a mesh: dp: 8 (over z, y), head: 4 (over x, core).
Axes of the slice: x: 2, y: 2, z: 4, core: 2. Of those that a mesh axis runs over, the one named last changes fastest.
Arguments:
- tokens: bfloat16 [32768, 512], P(('dp', 'head')), may hold values from -6 to 6
- segments: int32 [32768], P('dp'), may hold values from 0 to 255, never falling along the last dimension, each value on 1 to 256 neighbouring positions
- out_grad: bfloat16 [32768, 512], P(('dp', 'head')), may hold values from -6 to 6
- norm_params: float32 [4, 512], replicated, may hold values from -0.6 to 1.3
- norm_first: float32 [4, 512], replicated, may hold values from -0.0024414062 to 0.0024414062
- norm_second: float32 [4, 512], replicated, may hold values from 7.947286e-08 to 1.2715658e-06
- qkv_weight: float32 [512, 1536], P(None, 'head'), may hold values from -0.25 to 0.25
- qkv_moment: float32 [512, 1536], P(None, 'head'), may hold values from -0.0078125 to 0.0078125
- out_weight: float32 [512, 512], P('head'), may hold values from -2 to 2
- out_moment: float32 [512, 512], P('head'), may hold values from -0.0078125 to 0.0078125
- up_weight: float32 [512, 2048], P(None, ('dp', 'head')), may hold values from -0.25 to 0.25
- up_moment: float32 [512, 2048], P(None, ('dp', 'head')), may hold values from -0.0078125 to 0.0078125
- down_weight: float32 [512, 2048], P(None, ('dp', 'head')), may hold values from -0.125 to 0.125
- down_moment: float32 [512, 2048], P(None, ('dp', 'head')), may hold values from -0.0078125 to 0.0078125
Outputs:
- layer_out: bfloat16 [32768, 512], P(('dp', 'head'))
- input_grad: float32 [32768, 512], P(('dp', 'head'))
- grad_norm: float32 [], replicated
- clipped_grads: float32 [4, 512], replicated
- new_norm_first: float32 [4, 512], replicated
- new_norm_second: float32 [4, 512], replicated
- new_qkv_weight: float32 [512, 1536], P(None, 'head')
- new_qkv_moment: float32 [512, 1536], P(None, 'head')
- new_out_weight: float32 [512, 512], P('head')
- new_out_moment: float32 [512, 512], P('head')
- new_up_weight: float32 [512, 2048], P(None, ('dp', 'head'))
- new_up_moment: float32 [512, 2048], P(None, ('dp', 'head'))
- new_down_weight: float32 [512, 2048], P(None, ('dp', 'head'))
- new_down_moment: float32 [512, 2048], P(None, ('dp', 'head'))
Inputs may be any that keep to these rules, and one draw needn't show every extreme that they name: `segments`: segment ids never fall along the rows; each id covers 1 to 256 consecutive rows.
All inputs are finite; a program needn't handle non-finite values.
Results may differ from a plain program's by a relative error of at most 0.028.
Values may be sent and summed in bfloat16 or wider, within the bound.
A program may use at most 128 MiB of HBM per device.

v0:
```python
import math
import jax
import jax.numpy as jnp
from jax import lax
from jax.sharding import PartitionSpec as P

HEAD_DIM = 64
FF = 2048
SEQ = 512
NS_STEPS = 5
neg_fill = -1000000000.0
norm_eps = 1e-05
ns_a = 3.4445
ns_b = -4.775
ns_c = 2.0315
momentum_decay = 0.95
muon_rate = 0.5
muon_decay = 0.01
beta_one = 0.9
beta_two = 0.95


def normalize(values, gain, shift):
    mean = jnp.mean(values, axis=-1, keepdims=True)
    centered = values - mean
    factor = lax.rsqrt(jnp.mean(centered * centered, axis=-1, keepdims=True) + norm_eps)
    plain = centered * factor
    return (plain * gain + shift, plain, factor)


def normalize_back(upper, plain, factor, gain):
    inner = upper * gain
    lower = factor * (
        inner
        - jnp.mean(inner, axis=-1, keepdims=True)
        - plain * jnp.mean(inner * plain, axis=-1, keepdims=True)
    )
    return (lower, jnp.sum(upper * plain, axis=0), jnp.sum(upper, axis=0))


def masked_scores(query, keys, segment):
    scores = jnp.einsum(
        "qhd,khd->hqk", query, keys, preferred_element_type=jnp.float32
    ) * HEAD_DIM ** (-0.5)
    same = segment[:, None] == segment[None, :]
    return jnp.where(same[None], scores, neg_fill)


def attend_forward(block):
    query, keys, values, segment = block
    scores = masked_scores(query, keys, segment)
    top = jnp.max(scores, axis=-1, keepdims=True)
    weights = jnp.exp(scores - top)
    total = jnp.sum(weights, axis=-1, keepdims=True)
    probs = (weights / total).astype(jnp.bfloat16)
    context = jnp.einsum("hqk,khd->qhd", probs, values, preferred_element_type=jnp.float32)
    return (context.astype(jnp.bfloat16), top + jnp.log(total))


def attend_backward(block):
    query, keys, values, segment, context_grad, lse = block
    scores = masked_scores(query, keys, segment)
    probs = jnp.exp(scores - lse)
    probs_low = probs.astype(jnp.bfloat16)
    probs_grad = jnp.einsum(
        "qhd,khd->hqk", context_grad, values, preferred_element_type=jnp.float32
    )
    inner = jnp.sum(probs * probs_grad, axis=-1, keepdims=True)
    score_grad = (probs * (probs_grad - inner)).astype(jnp.bfloat16)
    query_grad = jnp.einsum(
        "hqk,khd->qhd", score_grad, keys, preferred_element_type=jnp.float32
    ) * HEAD_DIM ** (-0.5)
    key_grad = jnp.einsum(
        "hqk,qhd->khd", score_grad, query, preferred_element_type=jnp.float32
    ) * HEAD_DIM ** (-0.5)
    value_grad = jnp.einsum(
        "hqk,qhd->khd", probs_low, context_grad, preferred_element_type=jnp.float32
    )
    return jnp.stack([query_grad, key_grad, value_grad], axis=2).astype(jnp.bfloat16)


def gram_left(block):
    return lax.dot_general(
        block, block, (((1,), (1,)), ((), ())), preferred_element_type=jnp.float32
    )


def gram_right(block):
    return lax.dot_general(
        block, block, (((0,), (0,)), ((), ())), preferred_element_type=jnp.float32
    )


def squares_of(moment, grad, weight):
    return (
        jnp.stack([jnp.sum(moment * moment), jnp.sum(moment * grad), jnp.sum(grad * grad)]) * weight
    )


def shards(
    tokens,
    segments,
    out_grad,
    norm_params,
    norm_first,
    norm_second,
    qkv_weight,
    qkv_moment,
    out_weight,
    out_moment,
    up_weight,
    up_moment,
    down_weight,
    down_moment,
):
    width = tokens.shape[1]
    group = segments.shape[0]
    narrow = out_weight.shape[0]
    heads_here = narrow // HEAD_DIM
    sequences = group // SEQ
    inputs = tokens.astype(jnp.float32)
    first, first_plain, first_factor = normalize(inputs, norm_params[0], norm_params[1])
    first_all = lax.all_gather(first.astype(jnp.bfloat16), "head", axis=0, tiled=True)
    qkv_low = qkv_weight.astype(jnp.bfloat16)
    out_low = out_weight.astype(jnp.bfloat16)
    mixed = jnp.dot(first_all, qkv_low, preferred_element_type=jnp.float32).astype(jnp.bfloat16)
    mixed = mixed.reshape(sequences, SEQ, heads_here, 3, HEAD_DIM)
    segment_rows = segments.reshape(sequences, SEQ)
    query = mixed[:, :, :, 0]
    keys = mixed[:, :, :, 1]
    values = mixed[:, :, :, 2]
    context, lse = lax.map(attend_forward, (query, keys, values, segment_rows))
    context = context.reshape(group, narrow)
    context_rows = lax.all_to_all(context, "head", split_axis=0, concat_axis=1, tiled=True)
    out_full = lax.all_gather(out_low, "head", axis=0, tiled=True)
    attended = jnp.dot(context_rows, out_full, preferred_element_type=jnp.float32)
    middle = inputs + attended
    second, second_plain, second_factor = normalize(middle, norm_params[2], norm_params[3])
    second_low = second.astype(jnp.bfloat16)
    up_all, down_all = (
        lax.all_gather(up_weight.astype(jnp.bfloat16), ("dp", "head"), axis=1, tiled=True),
        lax.all_gather(down_weight.astype(jnp.bfloat16), ("dp", "head"), axis=1, tiled=True),
    )
    hidden = jnp.dot(second_low, up_all, preferred_element_type=jnp.float32)
    switch = jax.nn.sigmoid(1.702 * hidden)
    active = (hidden * switch).astype(jnp.bfloat16)
    result = middle + lax.dot_general(
        active, down_all, (((1,), (1,)), ((), ())), preferred_element_type=jnp.float32
    )
    layer_out = result.astype(jnp.bfloat16)
    down_grad = lax.dot_general(
        out_grad, active, (((0,), (0,)), ((), ())), preferred_element_type=jnp.float32
    )
    active_grad = jnp.dot(out_grad, down_all, preferred_element_type=jnp.float32)
    hidden_grad = (active_grad * (switch + 1.702 * hidden * switch * (1.0 - switch))).astype(
        jnp.bfloat16
    )
    up_grad = lax.dot_general(
        second_low, hidden_grad, (((0,), (0,)), ((), ())), preferred_element_type=jnp.float32
    )
    second_grad = lax.dot_general(
        hidden_grad, up_all, (((1,), (1,)), ((), ())), preferred_element_type=jnp.float32
    )
    up_part, down_part = (
        lax.psum_scatter(up_grad, ("dp", "head"), scatter_dimension=1, tiled=True),
        lax.psum_scatter(down_grad, ("dp", "head"), scatter_dimension=1, tiled=True),
    )
    middle_lower, gain_two, shift_two = normalize_back(
        second_grad, second_plain, second_factor, norm_params[2]
    )
    middle_grad = out_grad.astype(jnp.float32) + middle_lower
    attended_low = middle_grad.astype(jnp.bfloat16)
    rows_grad = lax.dot_general(
        attended_low, out_full, (((1,), (1,)), ((), ())), preferred_element_type=jnp.float32
    ).astype(jnp.bfloat16)
    context_grad = lax.all_to_all(rows_grad, "head", split_axis=1, concat_axis=0, tiled=True)
    whole_out = lax.dot_general(
        context_rows, attended_low, (((0,), (0,)), ((), ())), preferred_element_type=jnp.float32
    )
    out_part = lax.psum_scatter(
        whole_out.astype(jnp.bfloat16), "head", scatter_dimension=0, tiled=True
    )
    context_grad = context_grad.reshape(sequences, SEQ, heads_here, HEAD_DIM)
    mixed_grad = lax.map(attend_backward, (query, keys, values, segment_rows, context_grad, lse))
    mixed_grad = mixed_grad.reshape(group, 3 * narrow)
    qkv_part = lax.dot_general(
        first_all, mixed_grad, (((0,), (0,)), ((), ())), preferred_element_type=jnp.float32
    )
    mixed_rows = lax.all_to_all(mixed_grad, "head", split_axis=0, concat_axis=1, tiled=True)
    qkv_full = lax.all_gather(qkv_low, "head", axis=1, tiled=True)
    first_grad = lax.dot_general(
        mixed_rows, qkv_full, (((1,), (1,)), ((), ())), preferred_element_type=jnp.float32
    )
    input_lower, gain_one, shift_one = normalize_back(
        first_grad, first_plain, first_factor, norm_params[0]
    )
    input_grad = middle_grad + input_lower
    qkv_sum, out_sum = (
        lax.psum(qkv_part.astype(jnp.bfloat16), "dp").astype(jnp.float32),
        lax.psum(out_part, "dp").astype(jnp.float32),
    )
    leading = (lax.axis_index("dp") == 0).astype(jnp.float32)
    moments = [qkv_moment, out_moment, up_moment, down_moment]
    grads = [qkv_sum, out_sum, up_part, down_part]
    stats = jnp.stack(
        [
            squares_of(qkv_moment, qkv_sum, leading),
            squares_of(out_moment, out_sum, leading),
            squares_of(up_moment, up_part, 1.0),
            squares_of(down_moment, down_part, 1.0),
        ]
    )
    vector_part = jnp.stack([gain_one, shift_one, gain_two, shift_two])
    vector_sum, stat_sum = lax.psum((vector_part, stats), ("dp", "head"))
    grad_norm = jnp.sqrt(jnp.sum(stat_sum[:, 2]) + jnp.sum(vector_sum * vector_sum))
    clip = jnp.minimum(1.0, 1.0 / (grad_norm + 1e-06))
    sizes = jnp.sqrt(
        momentum_decay * momentum_decay * stat_sum[:, 0]
        + 2.0 * momentum_decay * clip * stat_sum[:, 1]
        + clip * clip * stat_sum[:, 2]
    )
    new_moments = [momentum_decay * moments[index] + clip * grads[index] for index in range(4)]
    starts = [
        (new_moments[index] / (sizes[index] + 1e-07)).astype(jnp.bfloat16) for index in range(4)
    ]
    up_block, down_block = (
        lax.all_gather(starts[2], "dp", axis=1, tiled=True),
        lax.all_gather(starts[3], "dp", axis=1, tiled=True),
    )
    blocks = [starts[0], starts[1], up_block, down_block]
    for turn in range(NS_STEPS):
        partials = (
            gram_left(blocks[0]),
            gram_right(blocks[1]),
            gram_left(blocks[2]),
            gram_left(blocks[3]),
        )
        grams = (
            lax.psum(partials[0].astype(jnp.bfloat16), "head").astype(jnp.float32),
            lax.psum(partials[1].astype(jnp.bfloat16), "head").astype(jnp.float32),
            lax.psum(partials[2].astype(jnp.bfloat16), "head").astype(jnp.float32),
            lax.psum(partials[3].astype(jnp.bfloat16), "head").astype(jnp.float32),
        )
        updated = []
        for index in range(4):
            gram = grams[index].astype(jnp.bfloat16)
            mix = (
                ns_b * gram.astype(jnp.float32)
                + ns_c * jnp.dot(gram, gram, preferred_element_type=jnp.float32)
            ).astype(jnp.bfloat16)
            if index == 1:
                product = jnp.dot(blocks[index], mix, preferred_element_type=jnp.float32)
            else:
                product = jnp.dot(mix, blocks[index], preferred_element_type=jnp.float32)
            updated.append(
                (ns_a * blocks[index].astype(jnp.float32) + product).astype(jnp.bfloat16)
            )
        blocks = updated
    share = up_weight.shape[1]
    offset = lax.axis_index("dp") * share
    owned = [
        blocks[0],
        blocks[1],
        lax.dynamic_slice_in_dim(blocks[2], offset, share, 1),
        lax.dynamic_slice_in_dim(blocks[3], offset, share, 1),
    ]
    weights = [qkv_weight, out_weight, up_weight, down_weight]
    factors = [
        math.sqrt(3.0),
        math.sqrt(SEQ / 8.0),
        math.sqrt(max(1.0, FF / width)),
        math.sqrt(max(1.0, FF / width)),
    ]
    new_weights = [
        weights[index] * (1.0 - muon_rate * muon_decay)
        - muon_rate * factors[index] * owned[index].astype(jnp.float32)
        for index in range(4)
    ]
    clipped = clip * vector_sum
    first_new = beta_one * norm_first + (1.0 - beta_one) * clipped
    second_new = beta_two * norm_second + (1.0 - beta_two) * clipped * clipped
    return (
        layer_out,
        input_grad,
        grad_norm,
        clipped,
        first_new,
        second_new,
        new_weights[0],
        new_moments[0],
        new_weights[1],
        new_moments[1],
        new_weights[2],
        new_moments[2],
        new_weights[3],
        new_moments[3],
    )


def solution(mesh):
    placed = (
        P(("dp", "head"), None),
        P("dp"),
        P(("dp", "head"), None),
        P(),
        P(),
        P(),
        P(None, "head"),
        P(None, "head"),
        P("head", None),
        P("head", None),
        P(None, ("dp", "head")),
        P(None, ("dp", "head")),
        P(None, ("dp", "head")),
        P(None, ("dp", "head")),
    )
    return jax.shard_map(
        shards,
        mesh=mesh,
        in_specs=placed,
        out_specs=(
            P(("dp", "head"), None),
            P(("dp", "head"), None),
            P(),
            P(),
            P(),
            P(),
            P(None, "head"),
            P(None, "head"),
            P("head", None),
            P("head", None),
            P(None, ("dp", "head")),
            P(None, ("dp", "head")),
            P(None, ("dp", "head")),
            P(None, ("dp", "head")),
        ),
        check_vma=False,
    )
```

profile of v0, /device:TPU:0, one launch (start us, length us, event | category | flops | bytes accessed | tf_op | source)
XLA Modules:
  0.0 1169.6 jit_solution(14758495943311568836)
XLA Ops:
  13.5 35.1 %all-gather.5.cloned.1.call-done = bf16[4096,512]{0,1:T(8,128)(2,1)} async-done(((bf16[1024,512]{0,1:T(8,128)(2,1)}), bf16[4096,512]{0,1:T(8,128)(2,1)}) %all-gather.5.cloned.1.call-update) | async-done | bytes 4194320 | tf_op jit(solution)/shard_map/all_gather | solution.py:123
  48.6 6.2 convolution_convert_fusion.2
  65.1 40.1 %while.22 = (s32[]{:T(128)}, bf16[8,512,2,64]{1,3,2,0:T(8,128)(2,1)}, f32[8,2,512,1]{2,1,3,0:T(2,128)}, bf16[8,512,2,64]{1,3,2,0:T(8,128)(2,1)}, s32[8,512]{1,0:...) while((s32[]{:T(128)}, ...), condition=%wide.region_5.6_spmd, body=%wide.region_2.5_spmd.sunk | while | flops 140835840 | bytes 7905881 | solution.py:132
  118.9 17.6 %all_gather.22 = bf16[512,512]{1,0:T(8,128)(2,1)} all-gather(bf16[128,512]{1,0:T(8,128)(2,1)S(1)} %convert_element_type.448), channel_id=1, replica_groups=mesh['dp'=8,'head'=4] {'head'}, dimensions={0}, use_global_device_ids=true | all-gather | bytes 655360 | tf_op jit(solution)/shard_map/all_gather | solution.py:135
  140.3 8.4 multiply_convert_fusion.2
  148.7 18.5 %all-gather.9.cloned.1.call-done = bf16[512,2048]{0,1:T(8,128)(2,1)} async-done(((bf16[512,64]{0,1:T(8,128)(2,1)}), bf16[512,2048]{0,1:T(8,128)(2,1)}) %all-gather.9.cloned.1.call-update) | async-done | bytes 2097168 | tf_op jit(solution)/shard_map/all_gather | solution.py:142
  167.2 8.4 multiply_convert_fusion.1
  197.5 11.2 all-to-all-done.1
  216.4 81.9 %while.23 = (s32[]{:T(128)}, bf16[8,512,2,3,64]{1,4,2,3,0:T(8,128)(2,1)}, bf16[8,512,2,64]{1,3,2,0:T(8,128)(2,1)}, s32[8,512]{1,0:T(8,128)}, bf16[8,512,2,64]{1,...) while((s32[]{:T(128)}, ...), condition=%wide.region_12.13_spmd, body=%wide.region_10.12_spmd.sunk | while | flops 342031360 | bytes 18380900 | solution.py:184
  309.2 7.3 fusion.263
  316.7 6.9 convolution_bitcast_fusion
  339.1 41.0 %all-reduce.14.cloned.1.call-done = (bf16[128,512]{1,0:T(8,128)(2,1)}, bf16[512,384]{1,0:T(8,128)(2,1)}) async-done(((bf16[128,512]{1,0:T(8,128)(2,1)}, bf16[512,384]{1,0:T(8,128)(2,1)}), (bf16[128,512]{1,0:T(8,128)(2,1)}, bf16[512,384]{1,0:T(8,128)(2,1)})) %all-reduce.14.cloned.1.call-update) | async-done | bytes 524304 | tf_op jit(solution)/shard_map/psum | solution.py:200
  388.8 12.2 %all-gather.11.cloned.1.call-done = bf16[512,1536]{1,0:T(8,128)(2,1)} async-done(((bf16[512,384]{1,0:T(8,128)(2,1)}), bf16[512,1536]{1,0:T(8,128)(2,1)}) %all-gather.11.cloned.1.call-update) | async-done | bytes 1572880 | tf_op jit(solution)/shard_map/all_gather | solution.py:190
  413.6 130.7 %reduce-scatter.6.cloned.1.call-done = f32[512,64]{0,1:T(8,128)} async-done(((f32[512,2048]{0,1:T(8,128)}), f32[512,64]{0,1:T(8,128)}) %reduce-scatter.6.cloned.1.call-update) | async-done | bytes 131088 | tf_op jit(solution)/shard_map/reduce_scatter | solution.py:165
  545.9 137.6 %reduce-scatter.8.cloned.1.call-done = f32[512,64]{0,1:T(8,128)} async-done(((f32[512,2048]{0,1:T(8,128)}), f32[512,64]{0,1:T(8,128)}) %reduce-scatter.8.cloned.1.call-update) | async-done | bytes 131088 | tf_op jit(solution)/shard_map/reduce_scatter | solution.py:166
  690.4 37.2 %all-reduce = (f32[4,3]{1,0:T(4,128)S(1)}, f32[4,512]{1,0:T(4,128)}) all-reduce(f32[4,3]{1,0:T(4,128)} %pad_maximum_fusion.1, f32[4,512]{1,0:T(4,128)} %pad_maximum_fusion), channel_id=1, replica_groups=mesh['dp'=8,'head'=4] {'dp','head'}, use_global_device_ids=true, to_apply=%region_32.33 | all-reduce | flops 2060 | bytes 16480 | tf_op jit(solution)/shard_map/psum | solution.py:214
  737.7 31.5 %all_gather.27 = bf16[512,512]{0,1:T(8,128)(2,1)S(1)} all-gather(bf16[512,64]{0,1:T(8,128)(2,1)S(1)} %get-tuple-element.241), channel_id=1, replica_groups=mesh['dp'=8,'head'=4] {'dp'}, dimensions={1}, use_global_device_ids=true | all-gather | bytes 589824 | tf_op jit(solution)/shard_map/all_gather | solution.py:228
  772.0 31.2 %all_gather.26 = bf16[512,512]{0,1:T(8,128)(2,1)S(1)} all-gather(bf16[512,64]{0,1:T(8,128)(2,1)S(1)} %get-tuple-element.243), channel_id=1, replica_groups=mesh['dp'=8,'head'=4] {'dp'}, dimensions={1}, use_global_device_ids=true | all-gather | bytes 589824 | tf_op jit(solution)/shard_map/all_gather | solution.py:227
  808.4 51.9 %all-reduce.24.cloned.1.call-done = (bf16[512,512]{1,0:T(8,128)(2,1)}, bf16[512,512]{1,0:T(8,128)(2,1)}, bf16[512,512]{1,0:T(8,128)(2,1)}, bf16[512,512]{1,0:T(8,128)(2,1)}) async-done(((bf16[512,512]{1,0:T(8,128)(2,1)}, bf16[512,512]{1,0:T(8,128)(2,1)}, bf16[512,512]{1,0:T(8,128)(2,1)}, bf16[512,512]{1,0:T(8,128)(2,1)}), (bf16[512,512]{1,0:T(8,128)(2,1)}, bf16[512,512]{1,0:T(8,128)(2,1)}, ...) | async-done | bytes 2097168 | tf_op jit(solution)/shard_map/psum | solution.py:239
  879.5 52.1 %all-reduce.22.cloned.1.call-done = (bf16[512,512]{1,0:T(8,128)(2,1)}, bf16[512,512]{1,0:T(8,128)(2,1)}, bf16[512,512]{1,0:T(8,128)(2,1)}, bf16[512,512]{1,0:T(8,128)(2,1)}) async-done(((bf16[512,512]{1,0:T(8,128)(2,1)}, bf16[512,512]{1,0:T(8,128)(2,1)}, bf16[512,512]{1,0:T(8,128)(2,1)}, bf16[512,512]{1,0:T(8,128)(2,1)}), (bf16[512,512]{1,0:T(8,128)(2,1)}, bf16[512,512]{1,0:T(8,128)(2,1)}, ...) | async-done | bytes 2097168 | tf_op jit(solution)/shard_map/psum | solution.py:239
  953.8 52.1 %all-reduce.20.cloned.1.call-done = (bf16[512,512]{1,0:T(8,128)(2,1)}, bf16[512,512]{1,0:T(8,128)(2,1)}, bf16[512,512]{1,0:T(8,128)(2,1)}, bf16[512,512]{1,0:T(8,128)(2,1)}) async-done(((bf16[512,512]{1,0:T(8,128)(2,1)}, bf16[512,512]{1,0:T(8,128)(2,1)}, bf16[512,512]{1,0:T(8,128)(2,1)}, bf16[512,512]{1,0:T(8,128)(2,1)}), (bf16[512,512]{1,0:T(8,128)(2,1)}, bf16[512,512]{1,0:T(8,128)(2,1)}, ...) | async-done | bytes 2097168 | tf_op jit(solution)/shard_map/psum | solution.py:239
  1025.1 6.8 add_convert_fusion
  1034.8 42.2 %all-reduce.18.cloned.1.call-done = (bf16[512,512]{1,0:T(8,128)(2,1)}, bf16[512,512]{1,0:T(8,128)(2,1)}, bf16[512,512]{1,0:T(8,128)(2,1)}, bf16[512,512]{1,0:T(8,128)(2,1)}) async-done(((bf16[512,512]{1,0:T(8,128)(2,1)}, bf16[512,512]{1,0:T(8,128)(2,1)}, bf16[512,512]{1,0:T(8,128)(2,1)}, bf16[512,512]{1,0:T(8,128)(2,1)}), (bf16[512,512]{1,0:T(8,128)(2,1)}, bf16[512,512]{1,0:T(8,128)(2,1)}, ...) | async-done | bytes 2097168 | tf_op jit(solution)/shard_map/psum | solution.py:239
  1103.8 44.4 %all-reduce.16.cloned.1.call-done = (bf16[512,512]{1,0:T(8,128)(2,1)}, bf16[512,512]{1,0:T(8,128)(2,1)}, bf16[512,512]{1,0:T(8,128)(2,1)}, bf16[512,512]{1,0:T(8,128)(2,1)}) async-done(((bf16[512,512]{1,0:T(8,128)(2,1)}, bf16[512,512]{1,0:T(8,128)(2,1)}, bf16[512,512]{1,0:T(8,128)(2,1)}, bf16[512,512]{1,0:T(8,128)(2,1)}), (bf16[512,512]{1,0:T(8,128)(2,1)}, bf16[512,512]{1,0:T(8,128)(2,1)}, ...) | async-done | bytes 2097168 | tf_op jit(solution)/shard_map/psum | solution.py:239
  (378 shorter events, 358.5 us)
Async XLA Ops:
  7.2 41.4 %all-gather.5.cloned.1.call-start = ((), (), s32[]{:S(2)}) async-start(), calls=%async_computation.6 | async-start | bytes 5242880 | tf_op jit(solution)/shard_map/all_gather | solution.py:123
  11.3 128.7 %all-gather.7.cloned.1.call-start = ((), (), s32[]{:S(2)}) async-start(), calls=%async_computation.7 | async-start | bytes 2162688 | tf_op jit(solution)/shard_map/all_gather | solution.py:141
  12.0 155.2 %all-gather.9.cloned.1.call-start = ((), (), s32[]{:S(2)}) async-start(), calls=%async_computation.8 | async-start | bytes 2162688 | tf_op jit(solution)/shard_map/all_gather | solution.py:142
  12.8 42.0 %copy-start.10 = (bf16[512,384]{1,0:T(8,128)(2,1)}, bf16[512,384]{1,0:T(8,128)(2,1)S(1)}, u32[]{:S(2)}) copy-start(bf16[512,384]{1,0:T(8,128)(2,1)S(1)} %convert_element_type.446) | copy-start | bytes 1179652
  113.8 22.7 %all-to-all-start = ((bf16[4,1024,128]{1,2,0:T(8,128)(2,1)}), bf16[4,1024,128]{1,2,0:T(8,128)(2,1)S(1)}, u32[]{:S(2)}, u32[]{:S(2)}) async-start(bf16[4,1024,128]{1,2,0:T(8,128)(2,1)} %copy.81), calls=%async_computation | async-start | bytes 2097152 | tf_op jit(solution)/shard_map/all_to_all | solution.py:134
  139.6 43.2 %copy-start = (f32[1024,512]{0,1:T(8,128)}, f32[1024,512]{0,1:T(8,128)S(1)}, u32[]{:S(2)}) copy-start(f32[1024,512]{0,1:T(8,128)S(1)} %get-tuple-element.263) | copy-start | bytes 6291460
  190.0 18.8 %all-to-all-start.1 = ((bf16[1024,4,128]{0,2,1:T(8,128)(2,1)}), bf16[1024,4,128]{0,2,1:T(8,128)(2,1)}, u32[]{:S(2)}, u32[]{:S(2)}) async-start(bf16[1024,4,128]{0,2,1:T(8,128)(2,1)} %bitcast.284), calls=%async_computation.1 | async-start | bytes 2097152 | tf_op jit(solution)/shard_map/all_to_all | solution.py:176
  194.2 114.3 %reduce-scatter.4.cloned.1.call-start = ((), (), s32[]{:S(2)}) async-start(), calls=%async_computation.10 | async-start | bytes 655360 | tf_op jit(solution)/shard_map/reduce_scatter | solution.py:180
  197.1 183.1 %all-reduce.14.cloned.1.call-start = ((), (), s32[]{:S(2)}) async-start(), calls=%async_computation.13 | async-start | bytes 1048576 | tf_op jit(solution)/shard_map/psum | solution.py:200
  308.6 92.4 %all-gather.11.cloned.1.call-start = ((), (), s32[]{:S(2)}) async-start(), calls=%async_computation.9 | async-start | bytes 1966080 | tf_op jit(solution)/shard_map/all_gather | solution.py:190
  309.1 235.2 %reduce-scatter.6.cloned.1.call-start = ((), (), s32[]{:S(2)}) async-start(), calls=%async_computation.11 | async-start | bytes 4325376 | tf_op jit(solution)/shard_map/reduce_scatter | solution.py:165
  316.5 367.0 %reduce-scatter.8.cloned.1.call-start = ((), (), s32[]{:S(2)}) async-start(), calls=%async_computation.12 | async-start | bytes 4325376 | tf_op jit(solution)/shard_map/reduce_scatter | solution.py:166
  334.2 50.5 %copy-start.12 = (f32[128,512]{1,0:T(8,128)S(1)}, f32[128,512]{1,0:T(8,128)}, u32[]{:S(2)}) copy-start(f32[128,512]{1,0:T(8,128)} %param.27) | copy-start | bytes 786436
  334.2 66.8 %all-to-all-start.2 = ((bf16[4,1024,384]{1,2,0:T(8,128)(2,1)}), bf16[4,1024,384]{1,2,0:T(8,128)(2,1)}, u32[]{:S(2)}, u32[]{:S(2)}) async-start(bf16[4,1024,384]{1,2,0:T(8,128)(2,1)} %copy.91), calls=%async_computation.2 | async-start | bytes 6291456 | tf_op jit(solution)/shard_map/all_to_all | solution.py:189
  339.1 521.2 %all-reduce.24.cloned.1.call-start = ((), (), s32[]{:S(2)}) async-start(), calls=%async_computation.18 | async-start | bytes 4194304 | tf_op jit(solution)/shard_map/psum | solution.py:239
  410.0 322.7 %copy-start.8 = (bf16[512,384]{1,0:T(8,128)(2,1)S(1)}, bf16[512,384]{1,0:T(8,128)(2,1)}, u32[]{:S(2)}) copy-start(bf16[512,384]{1,0:T(8,128)(2,1)} %get-tuple-element.220) | copy-start | bytes 1179652
  769.3 36.5 %copy-start.32 = (f32[128,512]{1,0:T(8,128)S(1)}, f32[128,512]{1,0:T(8,128)}, u32[]{:S(2)}) copy-start(f32[128,512]{1,0:T(8,128)} %fusion.219) | copy-start | bytes 786436
  808.2 123.5 %all-reduce.22.cloned.1.call-start = ((), (), s32[]{:S(2)}) async-start(), calls=%async_computation.17 | async-start | bytes 4194304 | tf_op jit(solution)/shard_map/psum | solution.py:239
  879.5 126.5 %all-reduce.20.cloned.1.call-start = ((), (), s32[]{:S(2)}) async-start(), calls=%async_computation.16 | async-start | bytes 4194304 | tf_op jit(solution)/shard_map/psum | solution.py:239
  953.8 123.2 %all-reduce.18.cloned.1.call-start = ((), (), s32[]{:S(2)}) async-start(), calls=%async_computation.15 | async-start | bytes 4194304 | tf_op jit(solution)/shard_map/psum | solution.py:239
  1024.8 123.3 %all-reduce.16.cloned.1.call-start = ((), (), s32[]{:S(2)}) async-start(), calls=%async_computation.14 | async-start | bytes 4194304 | tf_op jit(solution)/shard_map/psum | solution.py:239
  1099.6 48.6 %copy-start.42 = (bf16[512,512]{0,1:T(8,128)(2,1)S(1)}, bf16[512,512]{0,1:T(8,128)(2,1)}, u32[]{:S(2)}) copy-start(bf16[512,512]{0,1:T(8,128)(2,1)} %fusion.103) | copy-start | bytes 1572868
  1102.6 48.8 %copy-start.43 = (bf16[512,512]{0,1:T(8,128)(2,1)S(1)}, bf16[512,512]{0,1:T(8,128)(2,1)}, u32[]{:S(2)}) copy-start(bf16[512,512]{0,1:T(8,128)(2,1)} %fusion.99) | copy-start | bytes 1572868
  1103.2 50.5 %copy-start.34 = (f32[4,512]{1,0:T(4,128)}, f32[4,512]{1,0:T(4,128)S(1)}, u32[]{:S(2)}) copy-start(f32[4,512]{1,0:T(4,128)S(1)} %get-tuple-element.246) | copy-start | bytes 24580
  (44 other events, 289.8 us)
Sparse Core Ops, SparseCore 0:
  11.4 37.1 all-gather.4
  52.0 56.3 all-gather.6
  111.9 55.3 all-gather.8
  197.8 21.8 reduce-scatter.3
  308.7 71.3 all-reduce.13
  382.1 18.8 all-gather.10
  403.3 140.9 reduce-scatter.5
  546.6 136.9 reduce-scatter.7
  808.3 51.9 all-reduce.23
  879.6 51.9 all-reduce.21
  953.9 52.0 all-reduce.19
  1025.0 51.9 all-reduce.17
  1096.1 52.0 all-reduce.15
where the time goes:
time: 1180 us; the launch traced here: 1170 us
  waiting for transfers between devices  630 us (53%)
  matrix products  239 us (20%)
  blocking collectives  118 us (10%)
  local copies, waits for them, and re-layouts  78.6 us (7%)
  other arithmetic  69.6 us (6%)
  between operations  20.1 us (2%)
  starting transfers between devices  14.3 us (1%)
    psum x5, waiting for transfers between devices, shards(): lax.psum(partials[0].astype(jnp.bfloat16), 'head').astype(jnp.float32)  243 us
    reduce_scatter x1, waiting for transfers between devices, shards(): lax.psum_scatter(down_grad, ('dp', 'head'), scatter_dimension=1, tiled=True)  138 us
    reduce_scatter x1, waiting for transfers between devices, shards(): lax.psum_scatter(up_grad, ('dp', 'head'), scatter_dimension=1, tiled=True)  131 us
    dot_general x15, matrix products, shards(): product = jnp.dot(mix, blocks[index], preferred_element_type=jnp.float32)  45.7 us
    psum x1, waiting for transfers between devices, shards(): lax.psum(out_part, 'dp').astype(jnp.float32)  41 us
    psum x1, blocking collectives, shards(): vector_sum, stat_sum = lax.psum((vector_part, stats), ('dp', 'head'))  37.2 us
    all_gather x1, waiting for transfers between devices, shards(): lax.all_gather(first.astype(jnp.bfloat16), 'head', axis=0, tiled=True)  35.1 us
    all_gather x1, blocking collectives, shards(): lax.all_gather(starts[3], 'dp', axis=1, tiled=True)  31.5 us
  transfers between devices with their start and end apart: 16, of which 12 were waited for; matrix products, arithmetic and copies ran while one was open for 20% of the time, Pallas kernels for 0%

commit v1 on v0

--- a/solution.py
+++ b/solution.py
@@ -18,6 +18,28 @@
 muon_decay = 0.01
 beta_one = 0.9
 beta_two = 0.95
+
+
+def in_order(parts, dim):
+    dims = list(parts.shape[1:])
+    dims[dim] *= parts.shape[0]
+    return jnp.moveaxis(parts, 0, dim).reshape(dims)
+
+
+def collect(shard, axis, dim):
+    peers = lax.axis_size(axis)
+    pairs = [(i, (i + 1) % peers) for i in range(peers)]
+    back = [(b, a) for a, b in pairs]
+    lower, upper = ([], [])
+    for step in range(peers - 1):
+        if step % 2 == 0:
+            lower.append(lax.ppermute(lower[-1] if lower else shard, axis, pairs))
+        else:
+            upper.append(lax.ppermute(upper[-1] if upper else shard, axis, back))
+    parts = jnp.stack([*lower[::-1], shard, *upper])
+    shift = lax.axis_index(axis) - len(lower)
+    parts = parts[(jnp.arange(peers) - shift) % peers]
+    return in_order(parts, dim)
 
 
 def normalize(values, gain, shift):
@@ -225,7 +247,7 @@
     ]
     up_block, down_block = (
         lax.all_gather(starts[2], "dp", axis=1, tiled=True),
-        lax.all_gather(starts[3], "dp", axis=1, tiled=True),
+        collect(starts[3], "dp", 1),
     )
     blocks = [starts[0], starts[1], up_block, down_block]
     for turn in range(NS_STEPS):

time: 1180 us -> 1180 us (level)
  blocking collectives: 118 us -> 86 us
  starting transfers between devices: 14.3 us -> 28.6 us
    all_gather x1 -> x0, blocking collectives: 31.5 us -> none  [shards(): lax.all_gather(starts[3], 'dp', axis=1, tiled=True)]
    ppermute x0 -> x7, starting transfers between devices: none -> 14.3 us  [the longest x3 11.6 us: collect(): upper.append(lax.ppermute(upper[-1] if upper else shard, axis, back))]
  transfers between devices with their start and end apart: 16 -> 23, of which waited for: 12 -> 15; matrix products, arithmetic and copies ran while one was open for 20% -> 21% of each run, Pallas kernels for 0% -> 0%
where the time goes in v1:
time: 1180 us; the launch traced here: 1170 us
  waiting for transfers between devices  637 us (54%)
  matrix products  240 us (20%)
  local copies, waits for them, and re-layouts  87 us (7%)
  blocking collectives  86 us (7%)
  other arithmetic  68.8 us (6%)
  starting transfers between devices  28.6 us (2%)
  between operations  20.2 us (2%)
    psum x5, waiting for transfers between devices, shards(): lax.psum(partials[0].astype(jnp.bfloat16), 'head').astype(jnp.float32)  242 us
    reduce_scatter x1, waiting for transfers between devices, shards(): lax.psum_scatter(down_grad, ('dp', 'head'), scatter_dimension=1, tiled=True)  138 us
    reduce_scatter x1, waiting for transfers between devices, shards(): lax.psum_scatter(up_grad, ('dp', 'head'), scatter_dimension=1, tiled=True)  131 us
    dot_general x15, matrix products, shards(): product = jnp.dot(mix, blocks[index], preferred_element_type=jnp.float32)  45.7 us
    psum x1, waiting for transfers between devices, shards(): lax.psum(out_part, 'dp').astype(jnp.float32)  40.4 us
    psum x1, blocking collectives, shards(): vector_sum, stat_sum = lax.psum((vector_part, stats), ('dp', 'head'))  37.2 us
    all_gather x1, waiting for transfers between devices, shards(): lax.all_gather(first.astype(jnp.bfloat16), 'head', axis=0, tiled=True)  35.1 us
    all_gather x1, blocking collectives, shards(): lax.all_gather(starts[2], 'dp', axis=1, tiled=True)  31.2 us
  transfers between devices with their start and end apart: 23, of which 15 were waited for; matrix products, arithmetic and copies ran while one was open for 21% of the time, Pallas kernels for 0%

profile of v1, /device:TPU:0, one launch (start us, length us, event | category | flops | bytes accessed | tf_op | source)
XLA Modules:
  0.0 1168.1 jit_solution(6152565567794218936)
XLA Ops:
  13.5 35.1 %all-gather.5.cloned.1.call-done = bf16[4096,512]{0,1:T(8,128)(2,1)} async-done(((bf16[1024,512]{0,1:T(8,128)(2,1)}), bf16[4096,512]{0,1:T(8,128)(2,1)}) %all-gather.5.cloned.1.call-update) | async-done | bytes 4194320 | tf_op jit(solution)/shard_map/all_gather | solution.py:145
  48.6 6.2 convolution_convert_fusion.2
  65.1 40.1 %while.22 = (s32[]{:T(128)}, bf16[8,512,2,64]{1,3,2,0:T(8,128)(2,1)}, f32[8,2,512,1]{2,1,3,0:T(2,128)}, bf16[8,512,2,64]{1,3,2,0:T(8,128)(2,1)}, s32[8,512]{1,0:...) while((s32[]{:T(128)}, ...), condition=%wide.region_5.6_spmd, body=%wide.region_2.5_spmd.sunk | while | flops 140835840 | bytes 7905881 | solution.py:154
  118.9 17.6 %all_gather.19 = bf16[512,512]{1,0:T(8,128)(2,1)} all-gather(bf16[128,512]{1,0:T(8,128)(2,1)S(1)} %convert_element_type.448), channel_id=1, replica_groups=mesh['dp'=8,'head'=4] {'head'}, dimensions={0}, use_global_device_ids=true | all-gather | bytes 655360 | tf_op jit(solution)/shard_map/all_gather | solution.py:157
  140.3 8.4 multiply_convert_fusion.2
  148.7 18.5 %all-gather.9.cloned.1.call-done = bf16[512,2048]{0,1:T(8,128)(2,1)} async-done(((bf16[512,64]{0,1:T(8,128)(2,1)}), bf16[512,2048]{0,1:T(8,128)(2,1)}) %all-gather.9.cloned.1.call-update) | async-done | bytes 2097168 | tf_op jit(solution)/shard_map/all_gather | solution.py:164
  167.2 8.4 multiply_convert_fusion.1
  197.5 11.2 all-to-all-done.1
  216.5 82.0 %while.23 = (s32[]{:T(128)}, bf16[8,512,2,3,64]{1,4,2,3,0:T(8,128)(2,1)}, bf16[8,512,2,64]{1,3,2,0:T(8,128)(2,1)}, s32[8,512]{1,0:T(8,128)}, bf16[8,512,2,64]{1,...) while((s32[]{:T(128)}, ...), condition=%wide.region_12.13_spmd, body=%wide.region_10.12_spmd.sunk | while | flops 342031360 | bytes 18380900 | solution.py:206
  309.2 7.4 fusion.267
  316.9 6.8 convolution_bitcast_fusion
  339.8 40.4 %all-reduce.14.cloned.1.call-done = (bf16[128,512]{1,0:T(8,128)(2,1)}, bf16[512,384]{1,0:T(8,128)(2,1)}) async-done(((bf16[128,512]{1,0:T(8,128)(2,1)}, bf16[512,384]{1,0:T(8,128)(2,1)}), (bf16[128,512]{1,0:T(8,128)(2,1)}, bf16[512,384]{1,0:T(8,128)(2,1)})) %all-reduce.14.cloned.1.call-update) | async-done | bytes 524304 | tf_op jit(solution)/shard_map/psum | solution.py:222
  388.9 12.2 %all-gather.11.cloned.1.call-done = bf16[512,1536]{1,0:T(8,128)(2,1)} async-done(((bf16[512,384]{1,0:T(8,128)(2,1)}), bf16[512,1536]{1,0:T(8,128)(2,1)}) %all-gather.11.cloned.1.call-update) | async-done | bytes 1572880 | tf_op jit(solution)/shard_map/all_gather | solution.py:212
  401.1 6.1 fusion.273
  413.7 130.7 %reduce-scatter.6.cloned.1.call-done = f32[512,64]{0,1:T(8,128)} async-done(((f32[512,2048]{0,1:T(8,128)}), f32[512,64]{0,1:T(8,128)}) %reduce-scatter.6.cloned.1.call-update) | async-done | bytes 131088 | tf_op jit(solution)/shard_map/reduce_scatter | solution.py:187
  546.0 137.6 %reduce-scatter.8.cloned.1.call-done = f32[512,64]{0,1:T(8,128)} async-done(((f32[512,2048]{0,1:T(8,128)}), f32[512,64]{0,1:T(8,128)}) %reduce-scatter.8.cloned.1.call-update) | async-done | bytes 131088 | tf_op jit(solution)/shard_map/reduce_scatter | solution.py:188
  691.7 37.2 %all-reduce = (f32[4,3]{1,0:T(4,128)S(1)}, f32[4,512]{1,0:T(4,128)}) all-reduce(f32[4,3]{1,0:T(4,128)} %pad_maximum_fusion.1, f32[4,512]{1,0:T(4,128)} %pad_maximum_fusion), channel_id=1, replica_groups=mesh['dp'=8,'head'=4] {'dp','head'}, use_global_device_ids=true, to_apply=%region_32.33 | all-reduce | flops 2060 | bytes 16480 | tf_op jit(solution)/shard_map/psum | solution.py:236
  742.5 31.2 %all_gather.23 = bf16[512,512]{0,1:T(8,128)(2,1)S(1)} all-gather(bf16[512,64]{0,1:T(8,128)(2,1)S(1)} %get-tuple-element.243), channel_id=1, replica_groups=mesh['dp'=8,'head'=4] {'dp'}, dimensions={1}, use_global_device_ids=true | all-gather | bytes 589824 | tf_op jit(solution)/shard_map/all_gather | solution.py:249
  807.8 51.0 %all-reduce.24.cloned.1.call-done = (bf16[512,512]{1,0:T(8,128)(2,1)}, bf16[512,512]{1,0:T(8,128)(2,1)}, bf16[512,512]{1,0:T(8,128)(2,1)}, bf16[512,512]{1,0:T(8,128)(2,1)}) async-done(((bf16[512,512]{1,0:T(8,128)(2,1)}, bf16[512,512]{1,0:T(8,128)(2,1)}, bf16[512,512]{1,0:T(8,128)(2,1)}, bf16[512,512]{1,0:T(8,128)(2,1)}), (bf16[512,512]{1,0:T(8,128)(2,1)}, bf16[512,512]{1,0:T(8,128)(2,1)}, ...) | async-done | bytes 2097168 | tf_op jit(solution)/shard_map/psum | solution.py:261
  878.0 52.1 %all-reduce.22.cloned.1.call-done = (bf16[512,512]{1,0:T(8,128)(2,1)}, bf16[512,512]{1,0:T(8,128)(2,1)}, bf16[512,512]{1,0:T(8,128)(2,1)}, bf16[512,512]{1,0:T(8,128)(2,1)}) async-done(((bf16[512,512]{1,0:T(8,128)(2,1)}, bf16[512,512]{1,0:T(8,128)(2,1)}, bf16[512,512]{1,0:T(8,128)(2,1)}, bf16[512,512]{1,0:T(8,128)(2,1)}), (bf16[512,512]{1,0:T(8,128)(2,1)}, bf16[512,512]{1,0:T(8,128)(2,1)}, ...) | async-done | bytes 2097168 | tf_op jit(solution)/shard_map/psum | solution.py:261
  952.3 52.1 %all-reduce.20.cloned.1.call-done = (bf16[512,512]{1,0:T(8,128)(2,1)}, bf16[512,512]{1,0:T(8,128)(2,1)}, bf16[512,512]{1,0:T(8,128)(2,1)}, bf16[512,512]{1,0:T(8,128)(2,1)}) async-done(((bf16[512,512]{1,0:T(8,128)(2,1)}, bf16[512,512]{1,0:T(8,128)(2,1)}, bf16[512,512]{1,0:T(8,128)(2,1)}, bf16[512,512]{1,0:T(8,128)(2,1)}), (bf16[512,512]{1,0:T(8,128)(2,1)}, bf16[512,512]{1,0:T(8,128)(2,1)}, ...) | async-done | bytes 2097168 | tf_op jit(solution)/shard_map/psum | solution.py:261
  1023.4 6.8 add_convert_fusion
  1033.1 42.2 %all-reduce.18.cloned.1.call-done = (bf16[512,512]{1,0:T(8,128)(2,1)}, bf16[512,512]{1,0:T(8,128)(2,1)}, bf16[512,512]{1,0:T(8,128)(2,1)}, bf16[512,512]{1,0:T(8,128)(2,1)}) async-done(((bf16[512,512]{1,0:T(8,128)(2,1)}, bf16[512,512]{1,0:T(8,128)(2,1)}, bf16[512,512]{1,0:T(8,128)(2,1)}, bf16[512,512]{1,0:T(8,128)(2,1)}), (bf16[512,512]{1,0:T(8,128)(2,1)}, bf16[512,512]{1,0:T(8,128)(2,1)}, ...) | async-done | bytes 2097168 | tf_op jit(solution)/shard_map/psum | solution.py:261
  1102.1 44.4 %all-reduce.16.cloned.1.call-done = (bf16[512,512]{1,0:T(8,128)(2,1)}, bf16[512,512]{1,0:T(8,128)(2,1)}, bf16[512,512]{1,0:T(8,128)(2,1)}, bf16[512,512]{1,0:T(8,128)(2,1)}) async-done(((bf16[512,512]{1,0:T(8,128)(2,1)}, bf16[512,512]{1,0:T(8,128)(2,1)}, bf16[512,512]{1,0:T(8,128)(2,1)}, bf16[512,512]{1,0:T(8,128)(2,1)}), (bf16[512,512]{1,0:T(8,128)(2,1)}, bf16[512,512]{1,0:T(8,128)(2,1)}, ...) | async-done | bytes 2097168 | tf_op jit(solution)/shard_map/psum | solution.py:261
  (402 shorter events, 383.8 us)
Async XLA Ops:
  7.2 41.4 %all-gather.5.cloned.1.call-start = ((), (), s32[]{:S(2)}) async-start(), calls=%async_computation.6 | async-start | bytes 5242880 | tf_op jit(solution)/shard_map/all_gather | solution.py:145
  11.3 128.7 %all-gather.7.cloned.1.call-start = ((), (), s32[]{:S(2)}) async-start(), calls=%async_computation.7 | async-start | bytes 2162688 | tf_op jit(solution)/shard_map/all_gather | solution.py:163
  12.0 155.2 %all-gather.9.cloned.1.call-start = ((), (), s32[]{:S(2)}) async-start(), calls=%async_computation.8 | async-start | bytes 2162688 | tf_op jit(solution)/shard_map/all_gather | solution.py:164
  113.8 22.7 %all-to-all-start = ((bf16[4,1024,128]{1,2,0:T(8,128)(2,1)}), bf16[4,1024,128]{1,2,0:T(8,128)(2,1)S(1)}, u32[]{:S(2)}, u32[]{:S(2)}) async-start(bf16[4,1024,128]{1,2,0:T(8,128)(2,1)} %copy.81), calls=%async_computation | async-start | bytes 2097152 | tf_op jit(solution)/shard_map/all_to_all | solution.py:156
  190.0 18.8 %all-to-all-start.1 = ((bf16[1024,4,128]{0,2,1:T(8,128)(2,1)}), bf16[1024,4,128]{0,2,1:T(8,128)(2,1)}, u32[]{:S(2)}, u32[]{:S(2)}) async-start(bf16[1024,4,128]{0,2,1:T(8,128)(2,1)} %bitcast.309), calls=%async_computation.1 | async-start | bytes 2097152 | tf_op jit(solution)/shard_map/all_to_all | solution.py:198
  194.2 114.4 %reduce-scatter.4.cloned.1.call-start = ((), (), s32[]{:S(2)}) async-start(), calls=%async_computation.10 | async-start | bytes 655360 | tf_op jit(solution)/shard_map/reduce_scatter | solution.py:202
  197.1 183.2 %all-reduce.14.cloned.1.call-start = ((), (), s32[]{:S(2)}) async-start(), calls=%async_computation.13 | async-start | bytes 1048576 | tf_op jit(solution)/shard_map/psum | solution.py:222
  308.6 92.5 %all-gather.11.cloned.1.call-start = ((), (), s32[]{:S(2)}) async-start(), calls=%async_computation.9 | async-start | bytes 1966080 | tf_op jit(solution)/shard_map/all_gather | solution.py:212
  309.2 235.2 %reduce-scatter.6.cloned.1.call-start = ((), (), s32[]{:S(2)}) async-start(), calls=%async_computation.11 | async-start | bytes 4325376 | tf_op jit(solution)/shard_map/reduce_scatter | solution.py:187
  316.6 367.0 %reduce-scatter.8.cloned.1.call-start = ((), (), s32[]{:S(2)}) async-start(), calls=%async_computation.12 | async-start | bytes 4325376 | tf_op jit(solution)/shard_map/reduce_scatter | solution.py:188
  334.4 66.8 %all-to-all-start.2 = ((bf16[4,1024,384]{1,2,0:T(8,128)(2,1)}), bf16[4,1024,384]{1,2,0:T(8,128)(2,1)}, u32[]{:S(2)}, u32[]{:S(2)}) async-start(bf16[4,1024,384]{1,2,0:T(8,128)(2,1)} %copy.91), calls=%async_computation.2 | async-start | bytes 6291456 | tf_op jit(solution)/shard_map/all_to_all | solution.py:211
  339.2 519.7 %all-reduce.24.cloned.1.call-start = ((), (), s32[]{:S(2)}) async-start(), calls=%async_computation.18 | async-start | bytes 4194304 | tf_op jit(solution)/shard_map/psum | solution.py:261
  410.1 329.8 %copy-start.8 = (bf16[512,384]{1,0:T(8,128)(2,1)S(1)}, bf16[512,384]{1,0:T(8,128)(2,1)}, u32[]{:S(2)}) copy-start(bf16[512,384]{1,0:T(8,128)(2,1)} %get-tuple-element.220) | copy-start | bytes 1179652
  735.2 41.3 %collective-permute-start = (bf16[512,64]{0,1:T(8,128)(2,1)S(1)}, bf16[512,64]{0,1:T(8,128)(2,1)S(1)}, u32[]{:S(2)}, u32[]{:S(2)}) collective-permute-start(bf16[512,64]{0,1:T(8,128)(2,1)S(1)} %get-tuple-element.241), channel_id=1, source_target_pairs={{0,4},{4,8},{8,12},{12,16},{16,20},{20,24},{24,28},{28,0},{1,5},{5... | collective-permute-start | bytes 196616 | tf_op jit(solution)/shard_map/ppermute | solution.py:36
  737.8 46.5 %collective-permute-start.4 = (bf16[512,64]{0,1:T(8,128)(2,1)S(1)}, bf16[512,64]{0,1:T(8,128)(2,1)S(1)}, u32[]{:S(2)}, u32[]{:S(2)}) collective-permute-start(bf16[512,64]{0,1:T(8,128)(2,1)S(1)} %get-tuple-element.241), channel_id=1, source_target_pairs={{4,0},{8,4},{12,8},{16,12},{20,16},{24,20},{28,24},{0,28},{5,1},{9... | collective-permute-start | bytes 196616 | tf_op jit(solution)/shard_map/ppermute | solution.py:38
  776.5 7.0 collective-permute-start.1
  783.6 7.0 collective-permute-start.2
  784.3 7.4 collective-permute-start.5
  790.5 7.0 collective-permute-start.3
  791.7 10.3 collective-permute-start.6
  807.6 122.5 %all-reduce.22.cloned.1.call-start = ((), (), s32[]{:S(2)}) async-start(), calls=%async_computation.17 | async-start | bytes 4194304 | tf_op jit(solution)/shard_map/psum | solution.py:261
  877.9 126.5 %all-reduce.20.cloned.1.call-start = ((), (), s32[]{:S(2)}) async-start(), calls=%async_computation.16 | async-start | bytes 4194304 | tf_op jit(solution)/shard_map/psum | solution.py:261
  952.2 123.1 %all-reduce.18.cloned.1.call-start = ((), (), s32[]{:S(2)}) async-start(), calls=%async_computation.15 | async-start | bytes 4194304 | tf_op jit(solution)/shard_map/psum | solution.py:261
  1023.1 123.4 %all-reduce.16.cloned.1.call-start = ((), (), s32[]{:S(2)}) async-start(), calls=%async_computation.14 | async-start | bytes 4194304 | tf_op jit(solution)/shard_map/psum | solution.py:261
  (51 other events, 581.2 us)
Sparse Core Ops, SparseCore 0:
  11.4 37.1 all-gather.4
  52.0 56.3 all-gather.6
  111.9 55.3 all-gather.8
  197.8 21.9 reduce-scatter.3
  308.7 71.4 all-reduce.13
  382.2 18.8 all-gather.10
  403.4 140.9 reduce-scatter.5
  546.7 136.9 reduce-scatter.7
  807.7 51.1 all-reduce.23
  878.0 51.9 all-reduce.21
  952.3 52.0 all-reduce.19
  1023.3 51.9 all-reduce.17
  1094.5 52.0 all-reduce.15
